TPU v7x, 32 devices: a whole 2x2x4 slice. The times are simulated.
32 devices in a mesh: dp: 2 (over y), seq: 16 (over z, x, core).
Axes of the slice: x: 2, y: 2, z: 4, core: 2. Of those that a mesh axis runs over, the one named last changes fastest.
Arguments:
- tokens: bfloat16 [2, 4096, 768], P('dp', 'seq'), may hold values from -6 to 6
- segment_ids: int32 [2, 4096], P('dp', 'seq'), may hold values from 0 to 7, never falling along the last dimension, each value on 1 to 2048 neighbouring positions
- features: bfloat16 [12, 64, 256], replicated, may hold values from -6 to 6
- query_weight: bfloat16 [768, 768], replicated, may hold values from -0.15625 to 0.15625
- key_weight: bfloat16 [768, 768], replicated, may hold values from -0.15625 to 0.15625
- value_weight: bfloat16 [768, 768], replicated, may hold values from -0.21875 to 0.21875
- out_weight: bfloat16 [768, 768], replicated, may hold values from -0.875 to 0.875
- up_weight: bfloat16 [768, 3072], replicated, may hold values from -0.21875 to 0.21875
- down_weight: bfloat16 [3072, 768], replicated, may hold values from -0.109375 to 0.109375
- first_gain: float32 [768], replicated, may hold values from 0.1 to 1.9
- first_bias: float32 [768], replicated, may hold values from -3 to 3
- second_gain: float32 [768], replicated, may hold values from 0.1 to 1.9
- second_bias: float32 [768], replicated, may hold values from -3 to 3
- cotangent: bfloat16 [2, 4096, 768], P('dp', 'seq'), may hold values from -6 to 6
Outputs:
- output: bfloat16 [2, 4096, 768], P('dp', 'seq')
- grad_tokens: bfloat16 [2, 4096, 768], P('dp', 'seq')
- grad_query: float32 [768, 768], replicated
- grad_key: float32 [768, 768], replicated
- grad_value: float32 [768, 768], replicated
- grad_out: float32 [768, 768], replicated
- grad_up: float32 [768, 3072], replicated
- grad_down: float32 [3072, 768], replicated
- grad_first_gain: float32 [768], replicated
- grad_first_bias: float32 [768], replicated
- grad_second_gain: float32 [768], replicated
- grad_second_bias: float32 [768], replicated
Inputs may be any that keep to these rules, and one draw needn't show every extreme that they name: `segment_ids`: in each row the ids never fall, every id from 0 to 7 occurs, each on 1 to 2048 positions, and one on exactly 2048.
All inputs are finite; a program needn't handle non-finite values.
Results may differ from a plain program's by a relative error of at most 0.02.
Values sent between devices are 32-bit elements; how exact they have to be, the bound alone decides.
No kernel may reach another device: no remote copies, remote signals or barrier semaphores. Data moves between devices by JAX's collectives and lax.ppermute only.
A program may use at most 320 MiB of HBM per device.

v0:
```python
from functools import partial

import jax
import jax.numpy as jnp
from jax import lax
from jax.sharding import PartitionSpec as P

SEGS = 8


EPSILON = 1e-06
HIGHEST = lax.Precision.HIGHEST


def carried_in(value, axis, combine, identity, reverse):
    length, place = (lax.axis_size(axis), lax.axis_index(axis))
    everything = jax.tree.map(lambda part: lax.all_gather(part, axis), value)
    start = jax.tree.map(
        lambda part, zero: jnp.broadcast_to(jnp.asarray(zero, part.dtype), part.shape),
        value,
        identity,
    )

    def hop(k, before):
        at = length - 1 - k if reverse else k
        reached = at > place if reverse else at < place
        new = combine(before, jax.tree.map(lambda part: part[at], everything))
        return jax.tree.map(lambda a, b: jnp.where(reached, a, b), new, before)

    return lax.fori_loop(0, length, hop, start)


def norm_forward(hidden, norm_gain, norm_bias):
    row_mean = jnp.mean(hidden, -1, keepdims=True)
    centered = hidden - row_mean
    variance = jnp.mean(centered * centered, -1, keepdims=True)
    inv_std = lax.rsqrt(variance + EPSILON)
    normed = centered * inv_std
    return (normed * norm_gain + norm_bias, normed, inv_std)


def norm_backward(upstream, normed, inv_std, norm_gain):
    scaled = upstream * norm_gain
    grad_hidden = inv_std * (
        scaled
        - jnp.mean(scaled, -1, keepdims=True)
        - normed * jnp.mean(scaled * normed, -1, keepdims=True)
    )
    return (grad_hidden, jnp.sum(upstream * normed, 0), jnp.sum(upstream, 0))


def feature_map(projected, features):
    head_dim = projected.shape[-1]
    feat_count = features.shape[-1]
    inner_u = jnp.einsum("rthe,hem->rthm", projected, features, preferred_element_type=jnp.float32)
    widened = projected.astype(jnp.float32)
    square = jnp.sum(widened * widened, -1, keepdims=True)
    return jnp.exp(
        inner_u * head_dim ** (-0.25) - 0.5 * head_dim ** (-0.5) * square
    ) * feat_count ** (-0.5)


def feature_back(grad_feat, feat_vals, projected, features):
    head_dim = projected.shape[-1]
    weighted = grad_feat * feat_vals
    grad_inner = (weighted * head_dim ** (-0.25)).astype(jnp.bfloat16)
    grad_proj = jnp.einsum(
        "rthm,hem->rthe", grad_inner, features, preferred_element_type=jnp.float32
    )
    grad_proj = grad_proj - head_dim ** (-0.5) * projected.astype(jnp.float32) * jnp.sum(
        weighted, -1, keepdims=True
    )
    return grad_proj.astype(jnp.bfloat16)


def join_forward(earlier, later):
    earlier_kv, earlier_z, earlier_first, earlier_last, earlier_whole = earlier
    later_kv, later_z, later_first, later_last, later_whole = later
    matched = (earlier_last == later_first) | (earlier_last < 0) | (later_first < 0)
    joined = (later_whole == 1) & matched
    kv_part = jnp.where(joined[:, None, None, None], earlier_kv + later_kv, later_kv)
    z_part = jnp.where(joined[:, None, None], earlier_z + later_z, later_z)
    first_id = jnp.where(earlier_first < 0, later_first, earlier_first)
    last_id = jnp.where(later_last < 0, earlier_last, later_last)
    whole_run = earlier_whole * later_whole * matched.astype(jnp.int32)
    return (kv_part, z_part, first_id, last_id, whole_run)


def join_backward(earlier, later):
    earlier_kv, earlier_z, earlier_first, earlier_last, earlier_whole = earlier
    later_kv, later_z, later_first, later_last, later_whole = later
    matched = (later_last == earlier_first) | (later_last < 0) | (earlier_first < 0)
    joined = (later_whole == 1) & matched
    kv_part = jnp.where(joined[:, None, None, None], earlier_kv + later_kv, later_kv)
    z_part = jnp.where(joined[:, None, None], earlier_z + later_z, later_z)
    first_id = jnp.where(later_first < 0, earlier_first, later_first)
    last_id = jnp.where(earlier_last < 0, later_last, earlier_last)
    whole_run = earlier_whole * later_whole * matched.astype(jnp.int32)
    return (kv_part, z_part, first_id, last_id, whole_run)


def segment_totals(local_kv, local_z, segment_ids):
    row_count = local_kv.shape[0]
    labels = jnp.arange(local_kv.shape[1], dtype=jnp.int32)
    first_id = segment_ids[:, 0]
    last_id = segment_ids[:, -1]
    whole_run = (first_id == last_id).astype(jnp.int32)
    is_last = last_id[:, None] == labels[None, :]
    is_first = first_id[:, None] == labels[None, :]
    tail_kv = jnp.sum(jnp.where(is_last[:, :, None, None, None], local_kv, 0.0), 1)
    tail_z = jnp.sum(jnp.where(is_last[:, :, None, None], local_z, 0.0), 1)
    lead_kv = jnp.sum(jnp.where(is_first[:, :, None, None, None], local_kv, 0.0), 1)
    lead_z = jnp.sum(jnp.where(is_first[:, :, None, None], local_z, 0.0), 1)
    identity = (
        jnp.zeros_like(tail_kv),
        jnp.zeros_like(tail_z),
        -jnp.ones((row_count,), jnp.int32),
        -jnp.ones((row_count,), jnp.int32),
        jnp.ones((row_count,), jnp.int32),
    )
    before = carried_in(
        (tail_kv, tail_z, first_id, last_id, whole_run), "seq", join_forward, identity, False
    )
    behind = carried_in(
        (lead_kv, lead_z, first_id, last_id, whole_run), "seq", join_backward, identity, True
    )
    from_before = before[3][:, None] == labels[None, :]
    from_behind = behind[2][:, None] == labels[None, :]
    total_kv = (
        local_kv
        + jnp.where(from_before[:, :, None, None, None], before[0][:, None], 0.0)
        + jnp.where(from_behind[:, :, None, None, None], behind[0][:, None], 0.0)
    )
    total_z = (
        local_z
        + jnp.where(from_before[:, :, None, None], before[1][:, None], 0.0)
        + jnp.where(from_behind[:, :, None, None], behind[1][:, None], 0.0)
    )
    return (total_kv, total_z)


def body(
    tokens,
    segment_ids,
    features,
    query_weight,
    key_weight,
    value_weight,
    out_weight,
    up_weight,
    down_weight,
    first_gain,
    first_bias,
    second_gain,
    second_bias,
    cotangent,
):
    row_count, row_len, width_d = tokens.shape
    head_count, head_dim = (features.shape[0], features.shape[1])
    token_count = row_count * row_len
    tokens_flat = tokens.reshape(token_count, width_d)

    def project(weight):
        product = jnp.dot(tokens_flat, weight, preferred_element_type=jnp.float32)
        return product.astype(jnp.bfloat16).reshape(row_count, row_len, head_count, head_dim)

    queries = project(query_weight)
    keys_b = project(key_weight)
    values_b = project(value_weight)
    feat_q = feature_map(queries, features)
    feat_k = feature_map(keys_b, features)
    feat_q_b = feat_q.astype(jnp.bfloat16)
    feat_k_b = feat_k.astype(jnp.bfloat16)
    labels = jnp.arange(SEGS, dtype=jnp.int32)
    onehot = segment_ids[:, :, None] == labels[None, None, :]
    mask_b = onehot.astype(jnp.bfloat16)
    mask_f = onehot.astype(jnp.float32)
    masked_values = mask_b[:, :, :, None, None] * values_b[:, :, None]
    local_kv = jnp.einsum(
        "rthm,rtshe->rshme", feat_k_b, masked_values, preferred_element_type=jnp.float32
    )
    local_z = jnp.einsum("rts,rthm->rshm", mask_b, feat_k_b, preferred_element_type=jnp.float32)
    kv_total, z_total = segment_totals(local_kv, local_z, segment_ids)
    kv_b = kv_total.astype(jnp.bfloat16)
    per_segment = jnp.einsum(
        "rthm,rshme->rtshe", feat_q_b, kv_b, preferred_element_type=jnp.float32
    )
    numer = jnp.sum(jnp.where(onehot[:, :, :, None, None], per_segment, 0.0), 2)
    z_picked = jnp.einsum("rts,rshm->rthm", mask_f, z_total, precision=HIGHEST)
    denom = jnp.sum(feat_q_b.astype(jnp.float32) * z_picked, -1)
    attention = numer / denom[..., None]
    attention_b = attention.astype(jnp.bfloat16).reshape(token_count, width_d)
    hidden_one = tokens_flat.astype(jnp.float32) + jnp.dot(
        attention_b, out_weight, preferred_element_type=jnp.float32
    )
    normed_one, unit_one, inv_one = norm_forward(hidden_one, first_gain, first_bias)
    normed_one_b = normed_one.astype(jnp.bfloat16)
    inner_f = jnp.dot(normed_one_b, up_weight, preferred_element_type=jnp.float32)
    activated, gelu_pull = jax.vjp(partial(jax.nn.gelu, approximate=False), inner_f)
    activated_b = activated.astype(jnp.bfloat16)
    hidden_two = normed_one + jnp.dot(activated_b, down_weight, preferred_element_type=jnp.float32)
    result, unit_two, inv_two = norm_forward(hidden_two, second_gain, second_bias)
    upstream = cotangent.reshape(token_count, width_d).astype(jnp.float32)
    grad_two, grad_gain_two, grad_bias_two = norm_backward(upstream, unit_two, inv_two, second_gain)
    grad_branch = grad_two.astype(jnp.bfloat16)
    grad_down_w = jnp.einsum(
        "nf,nd->fd", activated_b, grad_branch, preferred_element_type=jnp.float32
    )
    grad_act = jnp.einsum("nd,fd->nf", grad_branch, down_weight, preferred_element_type=jnp.float32)
    (grad_inner,) = gelu_pull(grad_act)
    grad_inner_b = grad_inner.astype(jnp.bfloat16)
    grad_up_w = jnp.einsum(
        "nd,nf->df", normed_one_b, grad_inner_b, preferred_element_type=jnp.float32
    )
    grad_normed = grad_two + jnp.einsum(
        "nf,df->nd", grad_inner_b, up_weight, preferred_element_type=jnp.float32
    )
    grad_one, grad_gain_one, grad_bias_one = norm_backward(
        grad_normed, unit_one, inv_one, first_gain
    )
    grad_attn_out = grad_one.astype(jnp.bfloat16)
    grad_out_w = jnp.einsum(
        "nd,ne->de", attention_b, grad_attn_out, preferred_element_type=jnp.float32
    )
    grad_attention = jnp.einsum(
        "ne,de->nd", grad_attn_out, out_weight, preferred_element_type=jnp.float32
    )
    grad_attention = grad_attention.reshape(row_count, row_len, head_count, head_dim)
    grad_numer_b = (grad_attention / denom[..., None]).astype(jnp.bfloat16)
    grad_denom = -jnp.sum(grad_attention * attention, -1) / denom
    masked_grad = mask_b[:, :, :, None, None] * grad_numer_b[:, :, None]
    grad_feat_q = jnp.einsum(
        "rtshe,rshme->rthm", masked_grad, kv_b, preferred_element_type=jnp.float32
    )
    grad_feat_q = grad_feat_q + z_picked * grad_denom[..., None]
    local_grad_kv = jnp.einsum(
        "rthm,rtshe->rshme", feat_q_b, masked_grad, preferred_element_type=jnp.float32
    )
    local_grad_z = jnp.einsum(
        "rts,rthm->rshm",
        mask_f,
        feat_q_b.astype(jnp.float32) * grad_denom[..., None],
        precision=HIGHEST,
    )
    grad_kv_total, grad_z_total = segment_totals(local_grad_kv, local_grad_z, segment_ids)
    grad_kv_b = grad_kv_total.astype(jnp.bfloat16)
    grad_feat_k = jnp.einsum(
        "rtshe,rshme->rthm", masked_values, grad_kv_b, preferred_element_type=jnp.float32
    )
    grad_feat_k = grad_feat_k + jnp.einsum(
        "rts,rshm->rthm", mask_f, grad_z_total, precision=HIGHEST
    )
    value_terms = jnp.einsum(
        "rthm,rshme->rtshe", feat_k_b, grad_kv_b, preferred_element_type=jnp.float32
    )
    grad_values = jnp.sum(jnp.where(onehot[:, :, :, None, None], value_terms, 0.0), 2).astype(
        jnp.bfloat16
    )
    grad_queries = feature_back(grad_feat_q, feat_q, queries, features)
    grad_keys = feature_back(grad_feat_k, feat_k, keys_b, features)
    grad_q_flat = grad_queries.reshape(token_count, width_d)
    grad_k_flat = grad_keys.reshape(token_count, width_d)
    grad_v_flat = grad_values.reshape(token_count, width_d)
    grad_query_w = jnp.einsum(
        "nd,ne->de", tokens_flat, grad_q_flat, preferred_element_type=jnp.float32
    )
    grad_key_w = jnp.einsum(
        "nd,ne->de", tokens_flat, grad_k_flat, preferred_element_type=jnp.float32
    )
    grad_value_w = jnp.einsum(
        "nd,ne->de", tokens_flat, grad_v_flat, preferred_element_type=jnp.float32
    )
    grad_input = (
        grad_one
        + jnp.einsum("ne,de->nd", grad_q_flat, query_weight, preferred_element_type=jnp.float32)
        + jnp.einsum("ne,de->nd", grad_k_flat, key_weight, preferred_element_type=jnp.float32)
        + jnp.einsum("ne,de->nd", grad_v_flat, value_weight, preferred_element_type=jnp.float32)
    )
    local_grads = (
        grad_query_w,
        grad_key_w,
        grad_value_w,
        grad_out_w,
        grad_up_w,
        grad_down_w,
        grad_gain_one,
        grad_bias_one,
        grad_gain_two,
        grad_bias_two,
    )
    shares = (
        lax.psum_scatter(local_grads[0], "seq", scatter_dimension=0, tiled=True),
        lax.psum_scatter(local_grads[1], "seq", scatter_dimension=0, tiled=True),
        lax.psum_scatter(local_grads[2], "seq", scatter_dimension=0, tiled=True),
        lax.psum_scatter(local_grads[3], "seq", scatter_dimension=0, tiled=True),
        lax.psum_scatter(local_grads[4], "seq", scatter_dimension=0, tiled=True),
        lax.psum_scatter(local_grads[5], "seq", scatter_dimension=0, tiled=True),
        lax.psum_scatter(local_grads[6], "seq", scatter_dimension=0, tiled=True),
        lax.psum_scatter(local_grads[7], "seq", scatter_dimension=0, tiled=True),
        lax.psum_scatter(local_grads[8], "seq", scatter_dimension=0, tiled=True),
        lax.psum_scatter(local_grads[9], "seq", scatter_dimension=0, tiled=True),
    )
    shares = lax.psum(
        (
            shares[0],
            shares[1],
            shares[2],
            shares[3],
            shares[4],
            shares[5],
            shares[6],
            shares[7],
            shares[8],
            shares[9],
        ),
        "dp",
    )
    summed = (
        lax.all_gather(shares[0], "seq", axis=0, tiled=True),
        lax.all_gather(shares[1], "seq", axis=0, tiled=True),
        lax.all_gather(shares[2], "seq", axis=0, tiled=True),
        lax.all_gather(shares[3], "seq", axis=0, tiled=True),
        lax.all_gather(shares[4], "seq", axis=0, tiled=True),
        lax.all_gather(shares[5], "seq", axis=0, tiled=True),
        lax.all_gather(shares[6], "seq", axis=0, tiled=True),
        lax.all_gather(shares[7], "seq", axis=0, tiled=True),
        lax.all_gather(shares[8], "seq", axis=0, tiled=True),
        lax.all_gather(shares[9], "seq", axis=0, tiled=True),
    )
    return (
        result.astype(jnp.bfloat16).reshape(row_count, row_len, width_d),
        grad_input.astype(jnp.bfloat16).reshape(row_count, row_len, width_d),
        summed[0],
        summed[1],
        summed[2],
        summed[3],
        summed[4],
        summed[5],
        summed[6],
        summed[7],
        summed[8],
        summed[9],
    )


def solution(mesh):
    placed = (
        P("dp", "seq", None),
        P("dp", "seq"),
        P(),
        P(),
        P(),
        P(),
        P(),
        P(),
        P(),
        P(),
        P(),
        P(),
        P(),
        P("dp", "seq", None),
    )
    return jax.shard_map(
        body,
        mesh=mesh,
        in_specs=placed,
        out_specs=(
            P("dp", "seq", None),
            P("dp", "seq", None),
            P(),
            P(),
            P(),
            P(),
            P(),
            P(),
            P(),
            P(),
            P(),
            P(),
        ),
        check_vma=False,
    )
```

profile of v0, /device:TPU:0, one launch (start us, length us, event | category | flops | bytes accessed | tf_op | source)
XLA Modules:
  0.0 1851.8 jit_solution(2164421294902823707)
XLA Ops:
  17.5 5.5 fusion.14
  29.0 14.8 all-reduce.11
  51.6 21.3 %all-gather.9 = f32[16,12,256]{2,1,0:T(8,128)} all-gather(f32[1,12,256]{2,1,0:T(8,128)S(1)} %bitcast.471), channel_id=5, replica_groups=mesh['dp'=2,'seq'=16] {'seq'}, dimensions={0}, use_global_device_ids=true | all-gather | bytes 208896 | tf_op jit(solution)/shard_map/all_gather | solution.py:17
  73.0 22.4 %all-gather.8 = f32[16,12,256]{2,1,0:T(8,128)} all-gather(f32[1,12,256]{2,1,0:T(8,128)S(1)} %bitcast.470), channel_id=3, replica_groups=mesh['dp'=2,'seq'=16] {'seq'}, dimensions={0}, use_global_device_ids=true | all-gather | bytes 208896 | tf_op jit(solution)/shard_map/all_gather | solution.py:17
  98.3 31.5 %all-gather.37.cloned.1.call-done = f32[192,256,64]{1,2,0:T(8,128)} async-done(((f32[12,256,64]{1,2,0:T(8,128)}), f32[192,256,64]{1,2,0:T(8,128)}) %all-gather.37.cloned.1.call-update) | async-done | bytes 12582928 | tf_op jit(solution)/shard_map/all_gather | solution.py:17
  129.8 174.6 %while.77 = (s32[]{:T(128)}, f32[1,12,256,64]{3,2,1,0:T(8,128)}, f32[1,12,256]{2,1,0:T(8,128)}, s32[1]{0:T(128)}, s32[]{:T(128)}, /*index=5*/s32[16,1]{0,1:T(1,1...) while((s32[]{:T(128)}, f32[1,12,256,64]{3,2,1,0:T(8,128)}, ...), condition=%wide.region_8.9_spmd.clone, body=%wide.region_7.8_spmd.clone.sunk | while | flops 798738 | bytes 5640575 | solution.py:30
  156.5 2.8 fusion.225
  178.7 2.8 fusion.225
  222.6 2.9 fusion.225
  307.2 174.1 %while.76 = (s32[]{:T(128)}, f32[1,12,256,64]{3,2,1,0:T(8,128)}, f32[1,12,256]{2,1,0:T(8,128)S(1)}, s32[1]{0:T(128)}, s32[]{:T(128)}, /*index=5*/s32[16,1]{0,1:T...) while((s32[]{:T(128)}, f32[1,12,256,64]{3,2,1,0:T(8,128)}, ...), condition=%wide.region_4.5_spmd.clone, body=%wide.region_3.4_spmd.clone.sunk | while | flops 798734 | bytes 5542153 | solution.py:30
  483.2 4.4 fusion.31
  487.7 3.7 fusion.26
  494.5 8.1 multiply_convert_fusion.2
  506.3 3.6 add_convert_fusion
  514.3 5.5 fusion.10
  520.7 5.8 fusion.172
  529.6 3.4 copy.120
  535.3 22.8 %all-gather.11 = f32[16,12,256]{2,1,0:T(8,128)} all-gather(f32[1,12,256]{2,1,0:T(8,128)S(1)} %bitcast.469), channel_id=9, replica_groups=mesh['dp'=2,'seq'=16] {'seq'}, dimensions={0}, use_global_device_ids=true | all-gather | bytes 208896 | tf_op jit(solution)/shard_map/all_gather | solution.py:17
  558.1 20.9 %all-gather.10 = f32[16,12,256]{2,1,0:T(8,128)} all-gather(f32[1,12,256]{2,1,0:T(8,128)S(1)} %bitcast.468), channel_id=7, replica_groups=mesh['dp'=2,'seq'=16] {'seq'}, dimensions={0}, use_global_device_ids=true | all-gather | bytes 208896 | tf_op jit(solution)/shard_map/all_gather | solution.py:17
  579.1 42.0 %all-gather.41.cloned.1.call-done = f32[192,256,64]{1,2,0:T(8,128)} async-done(((f32[12,256,64]{1,2,0:T(8,128)}), f32[192,256,64]{1,2,0:T(8,128)}) %all-gather.41.cloned.1.call-update) | async-done | bytes 12582928 | tf_op jit(solution)/shard_map/all_gather | solution.py:17
  621.1 172.1 %while.79 = (s32[]{:T(128)}, f32[1,12,256,64]{3,2,1,0:T(8,128)}, f32[1,12,256]{2,1,0:T(8,128)}, s32[1]{0:T(128)}, s32[]{:T(128)}, /*index=5*/s32[16,1]{0,1:T(1,1...) while((s32[]{:T(128)}, f32[1,12,256,64]{3,2,1,0:T(8,128)}, ...), condition=%wide.region_29.30_spmd.clone, body=%wide.region_28.29_spmd.clone.sunk | while | flops 798738 | bytes 5640575 | solution.py:30
  647.4 2.8 fusion.231
  701.6 2.9 fusion.231
  723.3 2.8 fusion.231
  734.1 2.8 fusion.231
  766.7 2.8 fusion.231
  793.2 171.2 %while.78 = (s32[]{:T(128)}, f32[1,12,256,64]{3,2,1,0:T(8,128)}, f32[1,12,256]{2,1,0:T(8,128)S(1)}, s32[1]{0:T(128)}, s32[]{:T(128)}, /*index=5*/s32[16,1]{0,1:T...) while((s32[]{:T(128)}, f32[1,12,256,64]{3,2,1,0:T(8,128)}, ...), condition=%wide.region_25.26_spmd.clone, body=%wide.region_24.25_spmd.clone.sunk | while | flops 798734 | bytes 5542153 | solution.py:30
  970.3 4.2 fusion.32
  979.4 3.2 copy.122
  982.7 2.9 fusion.8
  988.2 3.2 copy.124
  993.8 6.8 fusion.156
  1002.4 6.1 fusion.116
  1010.3 34.6 %reduce-scatter.21.cloned.1.call-done = f32[48,768]{1,0:T(8,128)} async-done(((f32[768,768]{1,0:T(8,128)}), f32[48,768]{1,0:T(8,128)}) %reduce-scatter.21.cloned.1.call-update) | async-done | bytes 147472
  1046.8 64.8 %reduce-scatter.23.cloned.1.call-done = f32[48,768]{1,0:T(8,128)} async-done(((f32[768,768]{1,0:T(8,128)}), f32[48,768]{1,0:T(8,128)}) %reduce-scatter.23.cloned.1.call-update) | async-done | bytes 147472
  1113.4 64.8 %reduce-scatter.13.cloned.1.call-done = f32[48,768]{1,0:T(8,128)} async-done(((f32[768,768]{1,0:T(8,128)}), f32[48,768]{1,0:T(8,128)}) %reduce-scatter.13.cloned.1.call-update) | async-done | bytes 147472 | tf_op jit(solution)/shard_map/reduce_scatter | solution.py:295
  1178.2 115.0 %reduce-scatter.15.cloned.1.call-done = f32[48,3072]{1,0:T(8,128)} async-done(((f32[768,3072]{1,0:T(8,128)}), f32[48,3072]{1,0:T(8,128)}) %reduce-scatter.15.cloned.1.call-update) | async-done | bytes 589840 | tf_op jit(solution)/shard_map/reduce_scatter | solution.py:296
  1293.2 115.4 %reduce-scatter.17.cloned.1.call-done = f32[192,768]{1,0:T(8,128)} async-done(((f32[3072,768]{1,0:T(8,128)}), f32[192,768]{1,0:T(8,128)}) %reduce-scatter.17.cloned.1.call-update) | async-done | bytes 589840 | tf_op jit(solution)/shard_map/reduce_scatter | solution.py:297
  1408.7 74.8 %all-reduce.18.cloned.1.call-done = (f32[48,768]{0,1:T(8,128)}, f32[48,768]{0,1:T(8,128)}, f32[48,768]{0,1:T(8,128)}, f32[48,768]{1,0:T(8,128)}, f32[48,3072]{1,0:T(8,128)}, /*index=5*/f32[192,768]{1,0:T(8,128)}) async-done(((f32[48,768]{0,1:T(8,128)}, f32[48,768]{0,1:T(8,128)}, f32[48,768]{0,1:T(8,128)}, f32[48,768]{1,0:T(8,128)}, f32[48,3072]{1,0:T(8,128)}, /*index=5*/f32[192,768]{1,0:T(8,128)}), ...) | async-done | bytes 1769488 | tf_op jit(solution)/shard_map/psum | solution.py:303
  1493.3 61.7 %all-reduce.13 = (f32[768]{0:T(1024)}, f32[768]{0:T(1024)}, f32[768]{0:T(1024)}, f32[768]{0:T(1024)}) all-reduce(f32[768]{0:T(1024)S(1)} %copy-done.94, f32[768]{0:T(1024)S(1)} %copy-done.95, f32[768]{0:T(1024)S(1)} %copy-done.76, f32[768]{0:T(1024)S(1)} %convert_reduce_fusion), channel_id=16, replica_groups=mesh['dp'=2,'seq'=16] {'seq'}, use_global_device_ids=true, to_apply=%region_45.46.clone | all-reduce | flops 3072 | bytes 24576
  1558.0 5.4 all-reduce.14
  1566.8 58.2 %all-reduce.12 = (f32[768]{0:T(1024)}, f32[768]{0:T(1024)}, f32[768]{0:T(1024)}, f32[768]{0:T(1024)}) all-reduce(f32[768]{0:T(1024)S(1)} %dynamic-update-slice.3, f32[768]{0:T(1024)S(1)} %dynamic-update-slice.4, f32[768]{0:T(1024)S(1)} %dynamic-update-slice.5, f32[768]{0:T(1024)S(1)} %dynamic-update-slice.6), channel_id=1, replica_groups=mesh['dp'=2,'seq'=16] {'seq'}, use_global_device_ids=true, to_apply=%add.3 | all-reduce | flops 3072 | bytes 24576
  1627.8 32.4 %all-gather.29.cloned.1.call-done = f32[768,768]{1,0:T(8,128)} async-done(((f32[48,768]{1,0:T(8,128)}), f32[768,768]{1,0:T(8,128)}) %all-gather.29.cloned.1.call-update) | async-done | bytes 2359312 | tf_op jit(solution)/shard_map/all_gather | solution.py:322
  1660.1 81.8 %all-gather.31.cloned.1.call-done = f32[768,3072]{1,0:T(8,128)} async-done(((f32[48,3072]{1,0:T(8,128)}), f32[768,3072]{1,0:T(8,128)}) %all-gather.31.cloned.1.call-update) | async-done | bytes 9437200 | tf_op jit(solution)/shard_map/all_gather | solution.py:323
  1741.9 81.5 %all-gather.33.cloned.1.call-done = f32[3072,768]{1,0:T(8,128)} async-done(((f32[192,768]{1,0:T(8,128)}), f32[3072,768]{1,0:T(8,128)}) %all-gather.33.cloned.1.call-update) | async-done | bytes 9437200 | tf_op jit(solution)/shard_map/all_gather | solution.py:324
  1823.4 3.4 copy.211
  1833.0 3.7 copy.215
  1836.8 8.1 copy.216
  (842 shorter events, 558.6 us)
Async XLA Ops:
  7.2 485.4 %copy-start = (bf16[768,768]{1,0:T(8,128)(2,1)S(1)}, bf16[768,768]{1,0:T(8,128)(2,1)}, u32[]{:S(2)}) copy-start(bf16[768,768]{1,0:T(8,128)(2,1)} %param.28) | copy-start | bytes 3538948
  7.2 122.6 %all-gather.37.cloned.1.call-start = ((), (), s32[]{:S(2)}) async-start(), calls=%async_computation.16 | async-start | bytes 13369344 | tf_op jit(solution)/shard_map/all_gather | solution.py:17
  9.4 8.0 copy-start.13
  15.0 8.0 copy-start.81
  15.0 8.0 copy-start.84
  17.5 7.7 copy-start.98
  23.0 26.7 %copy-start.18 = (bf16[1,256,12,256]{1,3,2,0:T(8,128)(2,1)S(1)}, bf16[1,256,12,256]{1,3,2,0:T(8,128)(2,1)}, u32[]{:S(2)}) copy-start(bf16[1,256,12,256]{1,3,2,0:T(8,128)(2,1)} %copy-done.17) | copy-start | bytes 4718596
  23.0 284.1 %all-gather.35.cloned.1.call-start = ((), (), s32[]{:S(2)}) async-start(), calls=%async_computation.15 | async-start | bytes 13369344 | tf_op jit(solution)/shard_map/all_gather | solution.py:17
  23.8 597.3 %all-gather.41.cloned.1.call-start = ((), (), s32[]{:S(2)}) async-start(), calls=%async_computation.18 | async-start | bytes 13369344 | tf_op jit(solution)/shard_map/all_gather | solution.py:17
  47.5 50.9 %copy-start.15 = (f32[256,768]{0,1:T(8,128)}, f32[256,768]{0,1:T(8,128)S(1)}, u32[]{:S(2)}) copy-start(f32[256,768]{0,1:T(8,128)S(1)} %copy.83) | copy-start | bytes 2359300
  49.7 46.3 %copy-start.23 = (bf16[12,64,256]{2,1,0:T(8,128)(2,1)S(1)}, bf16[12,64,256]{2,1,0:T(8,128)(2,1)}, u32[]{:S(2)}) copy-start(bf16[12,64,256]{2,1,0:T(8,128)(2,1)} %param.24) | copy-start | bytes 1179652
  49.7 46.3 %copy-start.46 = (bf16[256,768]{0,1:T(8,128)(2,1)S(1)}, bf16[256,768]{0,1:T(8,128)(2,1)}, u32[]{:S(2)}) copy-start(bf16[256,768]{0,1:T(8,128)(2,1)} %copy.82) | copy-start | bytes 1179652
  152.1 7.3 copy-start.49
  174.2 7.3 copy-start.49
  185.3 7.2 copy-start.49
  207.2 7.2 copy-start.49
  218.2 7.4 copy-start.49
  251.3 7.2 copy-start.49
  262.2 7.2 copy-start.49
  491.4 22.7 %copy-start.52 = (f32[256,12]{0,1:T(8,128)}, f32[256,12]{0,1:T(8,128)S(1)}, u32[]{:S(2)}) copy-start(f32[256,12]{0,1:T(8,128)S(1)} %get-tuple-element.1168) | copy-start | bytes 36868
  491.4 22.8 %copy-start.20 = (bf16[1,256,12,256]{1,3,2,0:T(8,128)(2,1)}, bf16[1,256,12,256]{1,3,2,0:T(8,128)(2,1)S(1)}, u32[]{:S(2)}) copy-start(bf16[1,256,12,256]{1,3,2,0:T(8,128)(2,1)S(1)} %get-tuple-element.1169) | copy-start | bytes 4718596
  492.8 9.8 slice-start
  493.4 19.0 %copy-start.8 = (f32[256,768]{1,0:T(8,128)}, f32[256,768]{1,0:T(8,128)S(1)}, u32[]{:S(2)}) copy-start(f32[256,768]{1,0:T(8,128)S(1)} %get-tuple-element.1191) | copy-start | bytes 2359300
  493.4 19.0 %copy-start.70 = (f32[256]{0:T(256)}, f32[256]{0:T(256)S(1)}, u32[]{:S(2)}) copy-start(f32[256]{0:T(256)S(1)} %broadcast_multiply_fusion.9) | copy-start | bytes 3076
  494.5 17.9 copy-start.77
  494.5 8.1 slice-start.1
  519.8 273.4 %all-gather.39.cloned.1.call-start = ((), (), s32[]{:S(2)}) async-start(), calls=%async_computation.17 | async-start | bytes 13369344 | tf_op jit(solution)/shard_map/all_gather | solution.py:17
  520.4 488.1 %reduce-scatter.19.cloned.1.call-start = ((), (), s32[]{:S(2)}) async-start(), calls=%async_computation.19 | async-start | bytes 2506752
  579.1 465.9 %reduce-scatter.21.cloned.1.call-start = ((), (), s32[]{:S(2)}) async-start(), calls=%async_computation.20 | async-start | bytes 2506752
  982.6 129.0 %reduce-scatter.23.cloned.1.call-start = ((), (), s32[]{:S(2)}) async-start(), calls=%async_computation.21 | async-start | bytes 2506752
  991.4 186.7 %reduce-scatter.13.cloned.1.call-start = ((), (), s32[]{:S(2)}) async-start(), calls=%async_computation.9 | async-start | bytes 2506752 | tf_op jit(solution)/shard_map/reduce_scatter | solution.py:295
  993.7 299.5 %reduce-scatter.15.cloned.1.call-start = ((), (), s32[]{:S(2)}) async-start(), calls=%async_computation.11 | async-start | bytes 10027008 | tf_op jit(solution)/shard_map/reduce_scatter | solution.py:296
  1000.6 408.0 %reduce-scatter.17.cloned.1.call-start = ((), (), s32[]{:S(2)}) async-start(), calls=%async_computation.13 | async-start | bytes 10027008 | tf_op jit(solution)/shard_map/reduce_scatter | solution.py:297
  1008.4 475.0 %all-reduce.18.cloned.1.call-start = ((), (), s32[]{:S(2)}) async-start(), calls=%async_computation.22 | async-start | bytes 5013504 | tf_op jit(solution)/shard_map/psum | solution.py:303
  1408.6 84.7 %copy-start.76 = (f32[768]{0:T(1024)S(1)}, f32[768]{0:T(1024)}, u32[]{:S(2)}) copy-start(f32[768]{0:T(1024)} %get-tuple-element.1056) | copy-start | bytes 9220
  1408.6 84.7 %copy-start.94 = (f32[768]{0:T(1024)S(1)}, f32[768]{0:T(1024)}, u32[]{:S(2)}) copy-start(f32[768]{0:T(1024)} %get-tuple-element.1054) | copy-start | bytes 9220
  1408.6 84.7 %copy-start.95 = (f32[768]{0:T(1024)S(1)}, f32[768]{0:T(1024)}, u32[]{:S(2)}) copy-start(f32[768]{0:T(1024)} %get-tuple-element.1059) | copy-start | bytes 9220
  1408.6 216.3 %copy-start.25 = (bf16[768,768]{1,0:T(8,128)(2,1)S(1)}, bf16[768,768]{1,0:T(8,128)(2,1)}, u32[]{:S(2)}) copy-start(bf16[768,768]{1,0:T(8,128)(2,1)} %param.25) | copy-start | bytes 3538948
  1408.6 216.3 %copy-start.29 = (bf16[1,256,12,64]{1,3,2,0:T(8,128)(2,1)S(1)}, bf16[1,256,12,64]{1,3,2,0:T(8,128)(2,1)}, u32[]{:S(2)}) copy-start(bf16[1,256,12,64]{1,3,2,0:T(8,128)(2,1)} %copy-done.28) | copy-start | bytes 1179652
  1408.6 219.1 %all-gather.23.cloned.1.call-start = ((), (), s32[]{:S(2)}) async-start(), calls=%async_computation.6 | async-start | bytes 2506752 | tf_op jit(solution)/shard_map/all_gather | solution.py:319
  1485.3 142.4 %all-gather.25.cloned.1.call-start = ((), (), s32[]{:S(2)}) async-start(), calls=%async_computation.7 | async-start | bytes 2506752 | tf_op jit(solution)/shard_map/all_gather | solution.py:320
  1485.4 140.1 %copy-start.26 = (bf16[768,768]{1,0:T(8,128)(2,1)S(1)}, bf16[768,768]{1,0:T(8,128)(2,1)}, u32[]{:S(2)}) copy-start(bf16[768,768]{1,0:T(8,128)(2,1)} %param.26) | copy-start | bytes 3538948
  1487.3 140.5 %all-gather.27.cloned.1.call-start = ((), (), s32[]{:S(2)}) async-start(), calls=%async_computation.8 | async-start | bytes 2506752 | tf_op jit(solution)/shard_map/all_gather | solution.py:321
  1489.2 170.9 %all-gather.29.cloned.1.call-start = ((), (), s32[]{:S(2)}) async-start(), calls=%async_computation.10 | async-start | bytes 2506752 | tf_op jit(solution)/shard_map/all_gather | solution.py:322
  1489.8 252.1 %all-gather.31.cloned.1.call-start = ((), (), s32[]{:S(2)}) async-start(), calls=%async_computation.12 | async-start | bytes 10027008 | tf_op jit(solution)/shard_map/all_gather | solution.py:323
  1490.3 333.0 %all-gather.33.cloned.1.call-start = ((), (), s32[]{:S(2)}) async-start(), calls=%async_computation.14 | async-start | bytes 10027008 | tf_op jit(solution)/shard_map/all_gather | solution.py:324
  1627.7 199.0 %copy-start.40 = (f32[768,768]{1,0:T(8,128)S(1)}, f32[768,768]{1,0:T(8,128)}, u32[]{:S(2)}) copy-start(f32[768,768]{1,0:T(8,128)} %all-gather.25.cloned.1.call-done) | copy-start | bytes 7077892
  1836.7 8.1 copy-start.1
  (132 other events, 458.5 us)
Sparse Core Ops, SparseCore 0:
  23.1 106.6 all-gather.36
  132.6 98.5 all-gather.34
  519.9 101.1 all-gather.40
  623.2 99.1 all-gather.38
  726.5 61.4 reduce-scatter.18
  982.7 62.1 reduce-scatter.20
  1049.3 62.2 reduce-scatter.22
  1115.9 62.2 reduce-scatter.12
  1182.9 110.2 reduce-scatter.14
  1297.7 110.8 reduce-scatter.16
  1411.8 71.6 all-reduce.17
  1486.2 42.5 all-gather.22
  1531.7 41.1 all-gather.24
  1575.6 41.1 all-gather.26
  1618.9 41.1 all-gather.28
  1662.2 79.6 all-gather.30
  1744.0 79.3 all-gather.32
where the time goes:
time: 1870 us; the launch traced here: 1850 us
  waiting for transfers between devices  742 us (40%)
  other arithmetic  311 us (17%)
  local copies, waits for them, and re-layouts  263 us (14%)
  blocking collectives  227 us (12%)
  loops' own time  205 us (11%)
  matrix products  84.1 us (4%)
    select_n x128, other arithmetic, hop(): return jax.tree.map(lambda a, b: jnp.where(reached, a, b), new, before)  219 us
    another operation x4, loops' own time, carried_in(): return lax.fori_loop(0, length, hop, start)  205 us
    dynamic_slice x192, local copies, waits for them, and re-layouts, hop(): new = combine(before, jax.tree.map(lambda part: part[at], everything))  191 us
    unnamed x3, blocking collectives  135 us
    reduce_scatter x1, waiting for transfers between devices, body(): lax.psum_scatter(local_grads[5], 'seq', scatter_dimension=0, tiled=True)  115 us
    reduce_scatter x1, waiting for transfers between devices, body(): lax.psum_scatter(local_grads[4], 'seq', scatter_dimension=0, tiled=True)  115 us
    unnamed x20, waiting for transfers between devices  102 us
    all_gather x4, blocking collectives, carried_in(): everything = jax.tree.map(lambda part: lax.all_gather(part, axis), value)  87.4 us
  transfers between devices with their start and end apart: 17, of which 11 were waited for; matrix products, arithmetic and copies ran while one was open for 25% of the time, Pallas kernels for 0%

commit v1 on v0

v1 whole, which is shorter than its diff:
```python
from functools import partial

import jax
import jax.numpy as jnp
from jax import lax
from jax.experimental import pallas as pl
from jax.experimental.pallas import tpu as pltpu
from jax.sharding import PartitionSpec as P

SEG_MOST = 2048
EPSILON = 1e-06
QUAD = 4
NT = (((1,), (1,)), ((), ()))
NN = (((1,), (0,)), ((), ()))
TN = (((0,), (0,)), ((), ()))


def mxu(a, b, dims):
    return lax.dot_general(a, b, dims, preferred_element_type=jnp.float32)


def norm_forward(hidden, norm_gain, norm_bias):
    row_mean = jnp.mean(hidden, -1, keepdims=True)
    centered = hidden - row_mean
    variance = jnp.mean(centered * centered, -1, keepdims=True)
    inv_std = lax.rsqrt(variance + EPSILON)
    normed = centered * inv_std
    return (normed * norm_gain + norm_bias, normed, inv_std)


def norm_backward(upstream, normed, inv_std, norm_gain):
    scaled = upstream * norm_gain
    grad_hidden = inv_std * (
        scaled
        - jnp.mean(scaled, -1, keepdims=True)
        - normed * jnp.mean(scaled * normed, -1, keepdims=True)
    )
    return (grad_hidden, jnp.sum(upstream * normed, 0), jnp.sum(upstream, 0))


def features_of(rows, feats):
    head_dim, count = feats.shape
    wide = rows.astype(jnp.float32)
    square = jnp.sum(wide * wide, -1, keepdims=True)
    inner = mxu(rows, feats, NN)
    return jnp.exp(inner * head_dim ** (-0.25) - 0.5 * head_dim ** (-0.5) * square) * count ** (-0.5)


def features_back(weighted, rows, feats):
    head_dim = feats.shape[0]
    inner = (weighted * head_dim ** (-0.25)).astype(jnp.bfloat16)
    grad = mxu(inner, feats, NT)
    total = jnp.sum(weighted, -1, keepdims=True)
    return (grad - head_dim ** (-0.5) * rows.astype(jnp.float32) * total).astype(jnp.bfloat16)


class Plan:
    def __init__(self, heads, head_dim):
        self.heads, self.dim = heads, head_dim
        self.each = heads // QUAD
        self.block = self.each * head_dim + 8
        self.rows = QUAD * self.block

    def kv_row(self, head):
        return (head // self.each) * self.block + (head % self.each) * self.dim

    def z_row(self, head):
        return (head // self.each) * self.block + self.each * self.dim + head % self.each

    @property
    def first_row(self):
        return self.each * self.dim + self.each

    @property
    def last_row(self):
        return self.each * self.dim + self.each + 1


def put_state(plan, state_ref, head, pair_sum, z_lead, z_tail):
    at = pl.multiple_of(plan.kv_row(head), 8)
    state_ref[0, pl.ds(at, plan.dim), :] = pair_sum[: plan.dim]
    state_ref[1, pl.ds(at, plan.dim), :] = pair_sum[plan.dim :]
    z_at = plan.z_row(head)
    state_ref[0, pl.ds(z_at, 1), :] = z_lead
    state_ref[1, pl.ds(z_at, 1), :] = z_tail


def put_ids(plan, state_ref, seg_col):
    wide = state_ref.shape[2]
    length = seg_col.shape[0]
    first = jnp.broadcast_to(seg_col[0:1, :], (1, wide))
    last = jnp.broadcast_to(seg_col[length - 1 : length, :], (1, wide))
    for quarter in range(QUAD):
        base = quarter * plan.block
        state_ref[:, base + plan.block - 8 : base + plan.block, :] = jnp.zeros((2, 8, wide), jnp.float32)
        for side in range(2):
            state_ref[side, base + plan.first_row : base + plan.first_row + 1, :] = first
            state_ref[side, base + plan.last_row : base + plan.last_row + 1, :] = last


def get_carry(plan, carry_ref, head):
    at = pl.multiple_of(plan.kv_row(head), 8)
    z_at = plan.z_row(head)
    from_before = carry_ref[0, pl.ds(at, plan.dim), :]
    from_behind = carry_ref[1, pl.ds(at, plan.dim), :]
    both = jnp.concatenate([from_before, from_behind], 0).astype(jnp.bfloat16)
    return both, carry_ref[0, pl.ds(z_at, 1), :], carry_ref[1, pl.ds(z_at, 1), :]


def two_sided(rows, on_first, on_last):
    zero = jnp.zeros_like(rows)
    return jnp.concatenate([jnp.where(on_first, rows, zero), jnp.where(on_last, rows, zero)], 1)


def edges(seg_col):
    length = seg_col.shape[0]
    return seg_col == seg_col[0:1, :], seg_col == seg_col[length - 1 : length, :]


def project_kernel(plan, x_ref, wq_ref, wk_ref, wv_ref, feats_ref, seg_ref, q_ref, k_ref, v_ref, state_ref):
    step = pl.program_id(0)
    seg_col = seg_ref[...]

    @pl.when(step == 0)
    def _():
        put_ids(plan, state_ref, seg_col)

    x = x_ref[...]
    q_ref[...] = mxu(x, wq_ref[...], NN).astype(jnp.bfloat16)
    keys = mxu(x, wk_ref[...], NN).astype(jnp.bfloat16)
    values = mxu(x, wv_ref[...], NN).astype(jnp.bfloat16)
    k_ref[...] = keys
    v_ref[...] = values
    on_first, on_last = edges(seg_col)
    for i in range(2):
        lanes = slice(i * plan.dim, (i + 1) * plan.dim)
        feat_k = features_of(keys[:, lanes], feats_ref[i]).astype(jnp.bfloat16)
        sums = mxu(two_sided(values[:, lanes], on_first, on_last), feat_k, TN)
        wide = feat_k.astype(jnp.float32)
        z_lead = jnp.sum(jnp.where(on_first, wide, 0.0), 0, keepdims=True)
        z_tail = jnp.sum(jnp.where(on_last, wide, 0.0), 0, keepdims=True)
        put_state(plan, state_ref, 2 * step + i, sums, z_lead, z_tail)


def attend_kernel(plan, q_ref, k_ref, v_ref, feats_ref, seg_ref, row_ref, carry_ref, att_ref, attb_ref, den_ref):
    step = pl.program_id(0)
    seg_col = seg_ref[...]
    same = seg_col == row_ref[...]
    on_first, on_last = edges(seg_col)
    for i in range(2):
        lanes = slice(i * plan.dim, (i + 1) * plan.dim)
        fq = features_of(q_ref[:, lanes], feats_ref[i]).astype(jnp.bfloat16)
        fk = features_of(k_ref[:, lanes], feats_ref[i]).astype(jnp.bfloat16)
        both, z_before, z_behind = get_carry(plan, carry_ref, 2 * step + i)
        z_rows = jnp.where(on_first, z_before, 0.0) + jnp.where(on_last, z_behind, 0.0)
        scores = jnp.where(same, mxu(fq, fk, NT), 0.0)
        reach = mxu(fq, both, NT)
        numer = (
            mxu(scores.astype(jnp.bfloat16), v_ref[:, lanes], NN)
            + jnp.where(on_first, reach[:, : plan.dim], 0.0)
            + jnp.where(on_last, reach[:, plan.dim :], 0.0)
        )
        denom = jnp.sum(scores, -1, keepdims=True) + jnp.sum(
            fq.astype(jnp.float32) * z_rows, -1, keepdims=True
        )
        attention = numer / denom
        att_ref[:, lanes] = attention
        attb_ref[:, lanes] = attention.astype(jnp.bfloat16)
        den_ref[:, lanes] = jnp.broadcast_to(denom, attention.shape)


def pull_head(grad, attention, denom):
    grad_numer = (grad / denom).astype(jnp.bfloat16)
    grad_denom = -jnp.sum(grad * attention, -1, keepdims=True) / denom[:, :1]
    return grad_numer, grad_denom


def query_kernel(
    plan, q_ref, k_ref, v_ref, feats_ref, seg_ref, row_ref, carry_ref, grad_ref, att_ref, den_ref, dq_ref, state_ref
):
    step = pl.program_id(0)
    seg_col = seg_ref[...]

    @pl.when(step == 0)
    def _():
        put_ids(plan, state_ref, seg_col)

    same = seg_col == row_ref[...]
    on_first, on_last = edges(seg_col)
    for i in range(2):
        lanes = slice(i * plan.dim, (i + 1) * plan.dim)
        rows = q_ref[:, lanes]
        feat_q = features_of(rows, feats_ref[i])
        fq = feat_q.astype(jnp.bfloat16)
        fk = features_of(k_ref[:, lanes], feats_ref[i]).astype(jnp.bfloat16)
        both, z_before, z_behind = get_carry(plan, carry_ref, 2 * step + i)
        z_rows = jnp.where(on_first, z_before, 0.0) + jnp.where(on_last, z_behind, 0.0)
        grad_numer, grad_denom = pull_head(grad_ref[:, lanes], att_ref[:, lanes], den_ref[:, lanes])
        pulled = mxu(grad_numer, v_ref[:, lanes], NT) + grad_denom
        pulled = jnp.where(same, pulled, 0.0).astype(jnp.bfloat16)
        sides = two_sided(grad_numer, on_first, on_last)
        grad_feat = mxu(pulled, fk, NN) + mxu(sides, both, NN) + grad_denom * z_rows
        dq_ref[:, lanes] = features_back(grad_feat * feat_q, rows, feats_ref[i])
        sums = mxu(sides, fq, TN)
        scaled = fq.astype(jnp.float32) * grad_denom
        z_lead = jnp.sum(jnp.where(on_first, scaled, 0.0), 0, keepdims=True)
        z_tail = jnp.sum(jnp.where(on_last, scaled, 0.0), 0, keepdims=True)
        put_state(plan, state_ref, 2 * step + i, sums, z_lead, z_tail)


def key_kernel(
    plan, q_ref, k_ref, v_ref, feats_ref, seg_ref, row_ref, carry_ref, grad_ref, att_ref, den_ref, dk_ref, dv_ref
):
    step = pl.program_id(0)
    seg_col = seg_ref[...]
    same = seg_col == row_ref[...]
    on_first, on_last = edges(seg_col)
    for i in range(2):
        lanes = slice(i * plan.dim, (i + 1) * plan.dim)
        rows = k_ref[:, lanes]
        values = v_ref[:, lanes]
        fq = features_of(q_ref[:, lanes], feats_ref[i]).astype(jnp.bfloat16)
        feat_k = features_of(rows, feats_ref[i])
        fk = feat_k.astype(jnp.bfloat16)
        both, z_before, z_behind = get_carry(plan, carry_ref, 2 * step + i)
        grad_numer, grad_denom = pull_head(grad_ref[:, lanes], att_ref[:, lanes], den_ref[:, lanes])
        pulled = mxu(grad_numer, values, NT) + grad_denom
        pulled = jnp.where(same, pulled, 0.0).astype(jnp.bfloat16)
        scores = jnp.where(same, mxu(fk, fq, NT), 0.0).astype(jnp.bfloat16)
        grad_feat = (
            mxu(pulled, fq, TN)
            + mxu(two_sided(values, on_first, on_last), both, NN)
            + jnp.where(on_first, z_before, 0.0)
            + jnp.where(on_last, z_behind, 0.0)
        )
        reach = mxu(fk, both, NT)
        grad_values = (
            mxu(scores, grad_numer, NN)
            + jnp.where(on_first, reach[:, : plan.dim], 0.0)
            + jnp.where(on_last, reach[:, plan.dim :], 0.0)
        )
        dv_ref[:, lanes] = grad_values.astype(jnp.bfloat16)
        dk_ref[:, lanes] = features_back(grad_feat * feat_k, rows, feats_ref[i])


def exchange(plan, state, axis, row_len):
    count, place = lax.axis_size(axis), lax.axis_index(axis)
    block = plan.block

    def ids(part):
        first = part[0, plan.first_row, 0]
        last = part[0, plan.last_row, 0]
        return first, last

    def swap(part, bit):
        return lax.ppermute(part, axis, [(i, i ^ bit) for i in range(count)])

    def up(part, bit):
        high = (place // bit) % 2
        half = part.shape[1] // 2
        mine = lax.dynamic_slice_in_dim(part, high * half, half, 1)
        theirs = swap(lax.dynamic_slice_in_dim(part, (1 - high) * half, half, 1), bit)
        low = jnp.where(high == 0, mine, theirs)
        upper = jnp.where(high == 0, theirs, mine)
        (first_low, last_low), (first_up, last_up) = ids(low), ids(upper)
        lead = low[0] + jnp.where(first_low == first_up, upper[0], 0.0)
        tail = upper[1] + jnp.where(last_low == last_up, low[1], 0.0)
        return lead, tail, first_low, last_up, (low, upper)

    def mark(plan, lead, tail, first, last):
        rows = lax.broadcasted_iota(jnp.int32, (lead.shape[0], 1), 0) % block
        both = jnp.stack([lead, tail])
        both = jnp.where((rows == plan.first_row)[None], first, both)
        return jnp.where((rows == plan.last_row)[None], last, both)

    def down(carry, first, last, children, bit):
        low, upper = children
        high = (place // bit) % 2
        (first_low, last_low), (first_up, last_up) = ids(low), ids(upper)
        joined = last_low == first_up
        low_carry = jnp.stack(
            [carry[0], jnp.where(joined, upper[0], 0.0) + jnp.where(last_low == last, carry[1], 0.0)]
        )
        up_carry = jnp.stack(
            [jnp.where(joined, low[1], 0.0) + jnp.where(first_up == first, carry[0], 0.0), carry[1]]
        )
        mine = jnp.where(high == 0, low_carry, up_carry)
        theirs = swap(jnp.where(high == 0, up_carry, low_carry), bit)
        return jnp.concatenate(
            [jnp.where(high == 0, mine, theirs), jnp.where(high == 0, theirs, mine)], 1
        )

    lead, tail, first1, last1, children1 = up(state, 1)
    chip = mark(plan, lead, tail, first1, last1)
    lead, tail, first2, last2, children2 = up(chip, 2)
    quad = mark(plan, lead, tail, first2, last2)
    quads = count // QUAD
    reach = min(quads - 1, -(-SEG_MOST // (QUAD * row_len)))
    here = place // QUAD
    before = jnp.zeros_like(lead)
    behind = jnp.zeros_like(lead)
    for far in range(1, reach + 1):
        hop = far * QUAD
        lower = lax.ppermute(quad[1], axis, [(i, i + hop) for i in range(count - hop)])
        higher = lax.ppermute(quad[0], axis, [(i + hop, i) for i in range(count - hop)])
        low_last = lower[plan.last_row, 0]
        high_first = higher[plan.first_row, 0]
        before = before + jnp.where((here >= far) & (low_last == first2), lower, 0.0)
        behind = behind + jnp.where((here + far < quads) & (high_first == last2), higher, 0.0)
    carry = jnp.stack([before, behind])
    carry = down(carry, first2, last2, children2, 2)
    return down(carry, first1, last1, children1, 1)


def body(
    tokens,
    segment_ids,
    features,
    query_weight,
    key_weight,
    value_weight,
    out_weight,
    up_weight,
    down_weight,
    first_gain,
    first_bias,
    second_gain,
    second_bias,
    cotangent,
):
    row_count, row_len, width_d = tokens.shape
    head_count, head_dim, feat_count = features.shape
    plan = Plan(head_count, head_dim)
    x = tokens.reshape(row_count * row_len, width_d)
    seg = segment_ids.astype(jnp.float32)
    steps = head_count // 2
    lanes = 2 * head_dim

    pair = pl.BlockSpec((row_len, lanes), lambda p: (0, p))
    weight = pl.BlockSpec((width_d, lanes), lambda p: (0, p))
    feats = pl.BlockSpec((2, head_dim, feat_count), lambda p: (p, 0, 0))
    whole = lambda shape: pl.BlockSpec(shape, lambda p: (0,) * len(shape))
    col, row = whole((row_len, 1)), whole((1, row_len))
    state_shape = (2, plan.rows, feat_count)
    state = whole(state_shape)
    tall = lambda dtype: jax.ShapeDtypeStruct((row_len, width_d), dtype)
    state_out = jax.ShapeDtypeStruct(state_shape, jnp.float32)
    bf16, f32 = jnp.bfloat16, jnp.float32

    def call(kernel, ins, outs, shapes):
        return pl.pallas_call(
            partial(kernel, plan),
            grid=(steps,),
            in_specs=ins,
            out_specs=outs,
            out_shape=shapes,
            name=kernel.__name__,
            compiler_params=pltpu.CompilerParams(dimension_semantics=("arbitrary",)),
        )

    def per_row(work, *arrays):
        cut = lambda a, r: a[r * row_len : (r + 1) * row_len]
        done = [work(r, *[cut(a, r) for a in arrays]) for r in range(row_count)]
        if row_count == 1:
            return done[0]
        return tuple(jnp.concatenate(parts) for parts in zip(*done))

    kept = {}

    def attend(r, x_row):
        seg_col, seg_row = seg[r].reshape(row_len, 1), seg[r].reshape(1, row_len)
        queries, keys, values, own = call(
            project_kernel,
            [whole((row_len, width_d)), weight, weight, weight, feats, col],
            [pair, pair, pair, state],
            [tall(bf16), tall(bf16), tall(bf16), state_out],
        )(x_row, query_weight, key_weight, value_weight, features, seg_col)
        carry = exchange(plan, own, "seq", row_len)
        attention, attention_b, denom = call(
            attend_kernel,
            [pair, pair, pair, feats, col, row, state],
            [pair, pair, pair],
            [tall(f32), tall(bf16), tall(f32)],
        )(queries, keys, values, features, seg_col, seg_row, carry)
        kept[r] = (queries, keys, values, features, seg_col, seg_row, carry, attention, denom)
        return (attention_b,)

    (attention_b,) = per_row(attend, x)

    hidden_one = x.astype(f32) + jnp.dot(attention_b, out_weight, preferred_element_type=f32)
    normed_one, unit_one, inv_one = norm_forward(hidden_one, first_gain, first_bias)
    normed_one_b = normed_one.astype(bf16)
    inner_f = jnp.dot(normed_one_b, up_weight, preferred_element_type=f32)
    activated, gelu_pull = jax.vjp(partial(jax.nn.gelu, approximate=False), inner_f)
    activated_b = activated.astype(bf16)
    hidden_two = normed_one + jnp.dot(activated_b, down_weight, preferred_element_type=f32)
    result, unit_two, inv_two = norm_forward(hidden_two, second_gain, second_bias)
    upstream = cotangent.reshape(row_count * row_len, width_d).astype(f32)
    grad_two, grad_gain_two, grad_bias_two = norm_backward(upstream, unit_two, inv_two, second_gain)
    grad_branch = grad_two.astype(bf16)
    grad_down_w = mxu(activated_b, grad_branch, TN)
    (grad_inner,) = gelu_pull(mxu(grad_branch, down_weight, NT))
    grad_inner_b = grad_inner.astype(bf16)
    grad_up_w = mxu(normed_one_b, grad_inner_b, TN)
    grad_normed = grad_two + mxu(grad_inner_b, up_weight, NT)
    grad_one, grad_gain_one, grad_bias_one = norm_backward(grad_normed, unit_one, inv_one, first_gain)
    grad_attn_out = grad_one.astype(bf16)
    grad_out_w = mxu(attention_b, grad_attn_out, TN)
    grad_attention = mxu(grad_attn_out, out_weight, NT)

    def pull_back(r, grad_row):
        queries, keys, values, _, seg_col, seg_row, carry, attention, denom = kept[r]
        back_ins = [pair, pair, pair, feats, col, row, state, pair, pair, pair]
        first = (queries, keys, values, features, seg_col, seg_row)
        then = (grad_row, attention, denom)
        grad_q, own = call(query_kernel, back_ins, [pair, state], [tall(bf16), state_out])(*first, carry, *then)
        carry_back = exchange(plan, own, "seq", row_len)
        grad_k, grad_v = call(key_kernel, back_ins, [pair, pair], [tall(bf16), tall(bf16)])(
            *first, carry_back, *then
        )
        return grad_q, grad_k, grad_v

    grad_q, grad_k, grad_v = per_row(pull_back, grad_attention)
    grad_query_w = mxu(x, grad_q, TN)
    grad_key_w = mxu(x, grad_k, TN)
    grad_value_w = mxu(x, grad_v, TN)
    grad_input = (
        grad_one
        + mxu(grad_q, query_weight, NT)
        + mxu(grad_k, key_weight, NT)
        + mxu(grad_v, value_weight, NT)
    )
    grads = (
        grad_query_w,
        grad_key_w,
        grad_value_w,
        grad_out_w,
        grad_up_w,
        grad_down_w,
        grad_gain_one,
        grad_bias_one,
        grad_gain_two,
        grad_bias_two,
    )
    grads = lax.psum(grads, ("dp", "seq"))
    shape = (row_count, row_len, width_d)
    return (result.astype(bf16).reshape(shape), grad_input.astype(bf16).reshape(shape)) + tuple(grads)


def solution(mesh):
    tokens = P("dp", "seq", None)
    return jax.shard_map(
        body,
        mesh=mesh,
        in_specs=(tokens, P("dp", "seq")) + (P(),) * 11 + (tokens,),
        out_specs=(tokens, tokens) + (P(),) * 10,
        check_vma=False,
    )
```

time: 1870 us -> 723 us (0.39)
  waiting for transfers between devices: 742 us -> 417 us
  other arithmetic: 311 us -> 28.2 us
  local copies, waits for them, and re-layouts: 263 us -> 46.3 us
  loops' own time: 205 us -> 0 us
  blocking collectives: 227 us -> 40.9 us
  Pallas kernels: 0 us -> 59.9 us
  matrix products: 84.1 us -> 43.4 us
  starting transfers between devices: 0.94 us -> 39.1 us
  between operations: 18.4 us -> 46.3 us
    psum x1, waiting for transfers between devices: 74.8 us -> 385 us  [body(): grads = lax.psum(grads, ('dp', 'seq'))]
    reduce_scatter x3 -> x0, waiting for transfers between devices: 295 us -> none  [the longest x1 115 us: body(): lax.psum_scatter(local_grads[5], 'seq', scatter_dimension=0, tiled=True)]
    all_gather x10 -> x0, waiting for transfers between devices: 269 us -> none  [the longest x1 81.8 us: body(): lax.all_gather(shares[4], 'seq', axis=0, tiled=True)]
    another operation x4 -> x0, loops' own time: 205 us -> none  [carried_in(): return lax.fori_loop(0, length, hop, start)]
    select_n x128 -> x16, other arithmetic: 219 us -> 15.6 us  [the longest x4 6.78 us: mark(): return jnp.where((rows == plan.last_row)[None], last, both)]
    dynamic_slice x192 -> x4, local copies, waits for them, and re-layouts: 191 us -> 3.48 us  [up(): lax.dynamic_slice_in_dim(part, (1 - high) * half, half, 1)]
    unnamed x3 -> x0, blocking collectives: 135 us -> none
    unnamed x20 -> x1, waiting for transfers between devices: 102 us -> 0.02 us
  transfers between devices with their start and end apart: 17 -> 17, of which waited for: 11 -> 7; matrix products, arithmetic and copies ran while one was open for 25% -> 4% of each run, Pallas kernels for 0% -> 0%
where the time goes in v1:
time: 723 us; the launch traced here: 721 us
  waiting for transfers between devices  417 us (58%)
  Pallas kernels  59.9 us (8%)
  local copies, waits for them, and re-layouts  46.3 us (6%)
  between operations  46.3 us (6%)
  matrix products  43.4 us (6%)
  blocking collectives  40.9 us (6%)
  starting transfers between devices  39.1 us (5%)
  other arithmetic  28.2 us (4%)
    psum x1, waiting for transfers between devices, body(): grads = lax.psum(grads, ('dp', 'seq'))  385 us
    psum x1, blocking collectives, body(): grads = lax.psum(grads, ('dp', 'seq'))  40.9 us
    ppermute x8, waiting for transfers between devices, swap(): return lax.ppermute(part, axis, [(i, i ^ bit) for i in range(count)])  32.1 us
    dot_general x12, matrix products, mxu(): return lax.dot_general(a, b, dims, preferred_element_type=jnp.float32)  30.5 us
    unnamed x134, local copies, waits for them, and re-layouts  26.5 us
    ppermute x4, starting transfers between devices, exchange(): lax.ppermute(quad[1], axis, [(i, i + hop) for i in range(count - hop)])  25.4 us
    pallas_call x1, Pallas kernels, pull_back(): call(query_kernel, back_ins, [pair, state], [tall(bf16), state_out])  19.8 us
    pallas_call x1, Pallas kernels, pull_back(): call(key_kernel, back_ins, [pair, pair], [tall(bf16), tall(bf16)])  17.2 us
  transfers between devices with their start and end apart: 17, of which 7 were waited for; matrix products, arithmetic and copies ran while one was open for 4% of the time, Pallas kernels for 0%

profile of v1, /device:TPU:0, one launch (start us, length us, event | category | flops | bytes accessed | tf_op | source)
XLA Modules:
  0.0 721.0 jit_solution(11008122916556342972)
XLA Ops:
  7.2 1.3 fusion.76
  9.4 10.1 %project_kernel.1 = (bf16[256,768]{1,0:T(8,128)(2,1)}, bf16[256,768]{1,0:T(8,128)(2,1)}, bf16[256,768]{1,0:T(8,128)(2,1)}, f32[2,800,256]{2,1,0:T(8,128)}) custom-call(bf16[256,768]{1,0:T(8,128)(2,1)} %bitcast.133, bf16[768,768]{1,0:T(8,128)(2,1)} %wq_ref.1, bf16[768,768]{1,0:T(8,128)(2,1)} %wk_ref.1, bf16[768,768]{1,0:T(8,128)(2,1)} %wv_ref.1, ...), custom_call_target="tpu_custom_call" | custom-call | tf_op jit(solution)/shard_map/project_kernel/pallas_call | solution.py:372
  21.2 2.1 collective-permute-done
  23.3 1.6 dynamic-slice_select_fusion.2
  28.1 2.4 fusion.13
  31.5 2.9 collective-permute-start.1
  34.5 9.9 %collective-permute-done.1 = f32[2,200,256]{2,1,0:T(8,128)} collective-permute-done((f32[2,200,256]{2,1,0:T(8,128)S(1)}, f32[2,200,256]{2,1,0:T(8,128)}, u32[]{:S(2)}, u32[]{:S(2)}) %collective-permute-start.1) | collective-permute-done | bytes 409632 | tf_op jit(solution)/shard_map/ppermute | solution.py:256
  44.3 2.0 dynamic-slice_select_fusion.6
  51.8 1.4 fusion.26
  56.5 7.4 %collective-permute-start.3 = (f32[200,256]{1,0:T(8,128)S(1)}, f32[200,256]{1,0:T(8,128)}, u32[]{:S(2)}, u32[]{:S(2)}) collective-permute-start(f32[200,256]{1,0:T(8,128)S(1)} %get-tuple-element.136), channel_id=1, source_target_pairs={{0,8},{1,9},{2,10},{3,11},{4,12},{5,13},{6,14},{7,15},{16,24},{17,... | collective-permute-start | bytes 614408 | tf_op jit(solution)/shard_map/ppermute | solution.py:304
  63.9 5.3 collective-permute-start.2
  83.7 1.7 collective-permute-start.6
  88.1 5.6 collective-permute-done.6
  93.7 1.3 broadcast_select_fusion.7
  95.3 2.3 collective-permute-done.7
  99.1 12.8 %attend_kernel.1 = (f32[256,768]{1,0:T(8,128)}, bf16[256,768]{1,0:T(8,128)(2,1)}, f32[256,768]{1,0:T(8,128)}) custom-call(bf16[256,768]{1,0:T(8,128)(2,1)} %get-tuple-element.23.q_ref, bf16[256,768]{1,0:T(8,128)(2,1)} %get-tuple-element.24.k_ref, bf16[256,768]{1,0:T(8,128)(2,1)} %get-tuple-element.25.v_ref, bf16[12,64,256]{2,1,0:T(8,128)(2,1)} %feats_ref.7, ...), custom_call_target="tpu_custom_call" | custom-call | tf_op jit(solution)/shard_map/attend_kernel/pallas_call | solution.py:379
  111.9 1.7 fusion.77
  113.9 9.7 %multiply_convert_fusion = (bf16[256,3072]{1,0:T(8,128)(2,1)S(1)}, f32[256,3072]{1,0:T(8,128)S(1)}, f32[256,3072]{1,0:T(8,128)S(1)}) fusion(bf16[768,3072]{1,0:T(8,128)(2,1)} %param.21, f32[256,768]{1,0:T(8,128)S(1)} %get-tuple-element.145, f32[768]{0:T(1024)S(1)} %copy-done.33, f32[768]{0:T(1024)S(1)} %copy-done.31, f32[256]{0:T(256)S(1)} %add_rsqrt_fusion.1, ...), kind=kOutput, calls=%fused_computation.3 | convolution fusion | flops 1260060672 | bytes 13377536 | tf_op jit(solution)/shard_map/dot_general | solution.py:393
  123.6 1.5 fusion.78
  125.5 1.7 fusion.18
  127.3 3.8 add_convert_fusion
  131.2 2.4 multiply_reduce_fusion
  133.9 1.4 fusion.39.grad_ref
  135.3 19.8 %query_kernel.1 = (bf16[256,768]{1,0:T(8,128)(2,1)}, f32[2,800,256]{2,1,0:T(8,128)}) custom-call(bf16[256,768]{1,0:T(8,128)(2,1)} %get-tuple-element.23.q_ref, bf16[256,768]{1,0:T(8,128)(2,1)} %get-tuple-element.24.k_ref, bf16[256,768]{1,0:T(8,128)(2,1)} %get-tuple-element.25.v_ref, bf16[12,64,256]{2,1,0:T(8,128)(2,1)} %feats_ref.7, f32[256,1]{1,0:T(8,128)} %copy.29.seg_ref, ...), custom_call_target="tpu_custom_call" | custom-call | tf_op jit(solution)/shard_map/query_kernel/pallas_call | solution.py:416
  156.5 2.2 collective-permute-done.8
  165.9 1.5 fusion.14
  167.4 1.5 collective-permute-start.9
  169.0 10.1 %collective-permute-done.9 = f32[2,200,256]{2,1,0:T(8,128)S(1)} collective-permute-done((f32[2,200,256]{2,1,0:T(8,128)S(1)}, f32[2,200,256]{2,1,0:T(8,128)S(1)}, u32[]{:S(2)}, u32[]{:S(2)}) %collective-permute-start.9) | collective-permute-done | bytes 409632 | tf_op jit(solution)/shard_map/ppermute | solution.py:256
  184.2 1.5 fusion.27
  189.0 7.5 %collective-permute-start.11 = (f32[200,256]{1,0:T(8,128)S(1)}, f32[200,256]{1,0:T(8,128)}, u32[]{:S(2)}, u32[]{:S(2)}) collective-permute-start(f32[200,256]{1,0:T(8,128)S(1)} %get-tuple-element.126), channel_id=1, source_target_pairs={{0,8},{1,9},{2,10},{3,11},{4,12},{5,13},{6,14},{7,15},{16,24},{17,... | collective-permute-start | bytes 614408 | tf_op jit(solution)/shard_map/ppermute | solution.py:304
  196.4 5.3 collective-permute-start.10
  217.1 1.5 collective-permute-start.14
  218.5 5.3 fusion.59
  223.9 1.9 fusion.37
  230.7 1.9 convolution_bitcast_fusion.2
  232.7 5.5 fusion.41
  239.6 17.2 %key_kernel.1 = (bf16[256,768]{1,0:T(8,128)(2,1)}, bf16[256,768]{1,0:T(8,128)(2,1)}) custom-call(bf16[256,768]{1,0:T(8,128)(2,1)} %get-tuple-element.23.q_ref, bf16[256,768]{1,0:T(8,128)(2,1)} %get-tuple-element.24.k_ref, bf16[256,768]{1,0:T(8,128)(2,1)} %get-tuple-element.25.v_ref, bf16[12,64,256]{2,1,0:T(8,128)(2,1)} %feats_ref.7, f32[256,1]{1,0:T(8,128)} %copy.29.seg_ref, ...), custom_call_target="tpu_custom_call" | custom-call | tf_op jit(solution)/shard_map/key_kernel/pallas_call | solution.py:418
  256.8 3.0 convolution_bitcast_fusion.1
  259.8 1.9 convolution_bitcast_fusion
  262.4 40.9 %all-reduce = (f32[768]{0:T(1024)}, f32[768]{0:T(1024)}, f32[768]{0:T(1024)}, f32[768]{0:T(1024)}) all-reduce(f32[768]{0:T(1024)S(1)} %copy-done.51, f32[768]{0:T(1024)S(1)} %copy-done.52, f32[768]{0:T(1024)S(1)} %copy-done.41, f32[768]{0:T(1024)S(1)} %convert_reduce_fusion), channel_id=1, replica_groups=mesh['dp'=2,'seq'=16] {'dp','seq'}, use_global_device_ids=true, to_apply=%region_15.16 | all-reduce | flops 3072 | bytes 24576 | tf_op jit(solution)/shard_map/psum | solution.py:445
  303.3 1.6 convolution_add_fusion.2
  306.8 384.6 %all-reduce.4.cloned.1.call-done = (f32[768,768]{0,1:T(8,128)}, f32[768,768]{0,1:T(8,128)}, f32[768,768]{0,1:T(8,128)}, f32[768,768]{1,0:T(8,128)}, f32[768,3072]{1,0:T(8,128)}, /*index=5*/f32[3072,768]{1,0:T(8,128)}) async-done(((f32[768,768]{0,1:T(8,128)}, f32[768,768]{0,1:T(8,128)}, f32[768,768]{0,1:T(8,128)}, f32[768,768]{1,0:T(8,128)}, f32[768,3072]{1,0:T(8,128)}, /*index=5*/f32[3072,768]{1,0:T(8,128)}), ...) | async-done | bytes 28311568 | tf_op jit(solution)/shard_map/psum | solution.py:445
  691.3 3.2 copy.33
  694.5 1.9 copy.34
  696.5 3.2 copy.35
  699.7 1.4 copy.42
  701.1 9.3 %copy.43 = f32[768,3072]{1,0:T(8,128)} copy(f32[768,3072]{1,0:T(8,128)} %get-tuple-element.162) | data formatting | bytes 18874368
  710.4 3.7 copy.44
  (210 shorter events, 45.0 us)
Async XLA Ops:
  7.2 104.7 %copy-start = (bf16[768,768]{1,0:T(8,128)(2,1)S(1)}, bf16[768,768]{1,0:T(8,128)(2,1)}, u32[]{:S(2)}) copy-start(bf16[768,768]{1,0:T(8,128)(2,1)} %param.20) | copy-start | bytes 3538948
  7.2 684.1 %all-reduce.4.cloned.1.call-start = ((), (), s32[]{:S(2)}) async-start(), calls=%async_computation | async-start | bytes 56623104 | tf_op jit(solution)/shard_map/psum | solution.py:445
  20.7 2.6 collective-permute-start
  31.5 12.8 %collective-permute-start.1 = (f32[2,200,256]{2,1,0:T(8,128)S(1)}, f32[2,200,256]{2,1,0:T(8,128)}, u32[]{:S(2)}, u32[]{:S(2)}) collective-permute-start(f32[2,200,256]{2,1,0:T(8,128)S(1)} %constant_dynamic-slice_fusion.2), channel_id=1, source_target_pairs={{0,2},{1,3},{2,0},{3,1},{4,6},{5,7},{6,4},{7,5},{8,10},{9,11},{10,... | collective-permute-start | bytes 1228808 | tf_op jit(solution)/shard_map/ppermute | solution.py:256
  34.4 17.3 %copy-start.53 = (pred[200]{0:T(512)(128)(4,1)}, pred[200]{0:T(512)(128)(4,1)S(1)}, u32[]{:S(2)}) copy-start(pred[200]{0:T(512)(128)(4,1)S(1)} %get-tuple-element.154) | copy-start | bytes 604
  34.5 17.3 %copy-start.55 = (pred[200]{0:T(512)(128)(4,1)}, pred[200]{0:T(512)(128)(4,1)S(1)}, u32[]{:S(2)}) copy-start(pred[200]{0:T(512)(128)(4,1)S(1)} %get-tuple-element.155) | copy-start | bytes 604
  53.9 17.9 %collective-permute-start.5 = (f32[200,256]{1,0:T(8,128)}, f32[200,256]{1,0:T(8,128)}, u32[]{:S(2)}, u32[]{:S(2)}) collective-permute-start(f32[200,256]{1,0:T(8,128)} %get-tuple-element.137), channel_id=1, source_target_pairs={{8,0},{9,1},{10,2},{11,3},{12,4},{13,5},{14,6},{15,7},{24,16},{25,... | collective-permute-start | bytes 614408 | tf_op jit(solution)/shard_map/ppermute | solution.py:305
  55.2 19.1 %collective-permute-start.4 = (f32[200,256]{1,0:T(8,128)}, f32[200,256]{1,0:T(8,128)}, u32[]{:S(2)}, u32[]{:S(2)}) collective-permute-start(f32[200,256]{1,0:T(8,128)} %get-tuple-element.137), channel_id=1, source_target_pairs={{4,0},{5,1},{6,2},{7,3},{8,4},{9,5},{10,6},{11,7},{12,8},{13,9},{1... | collective-permute-start | bytes 614408 | tf_op jit(solution)/shard_map/ppermute | solution.py:305
  56.5 20.3 %collective-permute-start.3 = (f32[200,256]{1,0:T(8,128)S(1)}, f32[200,256]{1,0:T(8,128)}, u32[]{:S(2)}, u32[]{:S(2)}) collective-permute-start(f32[200,256]{1,0:T(8,128)S(1)} %get-tuple-element.136), channel_id=1, source_target_pairs={{0,8},{1,9},{2,10},{3,11},{4,12},{5,13},{6,14},{7,15},{16,24},{17,... | collective-permute-start | bytes 614408 | tf_op jit(solution)/shard_map/ppermute | solution.py:304
  63.9 15.4 %collective-permute-start.2 = (f32[200,256]{1,0:T(8,128)S(1)}, f32[200,256]{1,0:T(8,128)}, u32[]{:S(2)}, u32[]{:S(2)}) collective-permute-start(f32[200,256]{1,0:T(8,128)S(1)} %get-tuple-element.136), channel_id=1, source_target_pairs={{0,4},{1,5},{2,6},{3,7},{4,8},{5,9},{6,10},{7,11},{8,12},{9,13},{1... | collective-permute-start | bytes 614408 | tf_op jit(solution)/shard_map/ppermute | solution.py:304
  83.7 9.9 %collective-permute-start.6 = (f32[2,200,256]{2,1,0:T(8,128)S(1)}, f32[2,200,256]{2,1,0:T(8,128)}, u32[]{:S(2)}, u32[]{:S(2)}) collective-permute-start(f32[2,200,256]{2,1,0:T(8,128)S(1)} %fusion.31), channel_id=1, source_target_pairs={{0,2},{1,3},{2,0},{3,1},{4,6},{5,7},{6,4},{7,5},{8,10},{9,11},{10,... | collective-permute-start | bytes 1228808 | tf_op jit(solution)/shard_map/ppermute | solution.py:256
  95.2 2.4 collective-permute-start.7
  97.8 14.1 %copy-start.2 = (bf16[1,256,768]{2,1,0:T(8,128)(2,1)S(1)}, bf16[1,256,768]{2,1,0:T(8,128)(2,1)}, u32[]{:S(2)}) copy-start(bf16[1,256,768]{2,1,0:T(8,128)(2,1)} %param.14) | copy-start | bytes 1179652
  99.1 14.8 %copy-start.31 = (f32[768]{0:T(1024)S(1)}, f32[768]{0:T(1024)}, u32[]{:S(2)}) copy-start(f32[768]{0:T(1024)} %param.23) | copy-start | bytes 9220
  99.1 14.8 %copy-start.33 = (f32[768]{0:T(1024)S(1)}, f32[768]{0:T(1024)}, u32[]{:S(2)}) copy-start(f32[768]{0:T(1024)} %param.24) | copy-start | bytes 9220
  111.9 11.7 %slice-start.3 = ((s8[4718592]{0:T(1024)(128)(4,1)}), s8[4194304]{0:T(1024)(128)(4,1)S(1)}, s32[]{:S(2)}) async-start(s8[4718592]{0:T(1024)(128)(4,1)} %bitcast.136), calls=%async_computation.4 | async-start | bytes 8388608
  113.6 20.0 %copy-start.35 = (f32[256]{0:T(256)}, f32[256]{0:T(256)S(1)}, u32[]{:S(2)}) copy-start(f32[256]{0:T(256)S(1)} %broadcast_multiply_fusion.5) | copy-start | bytes 3076
  113.9 19.7 %copy-start.42 = (f32[256]{0:T(256)}, f32[256]{0:T(256)S(1)}, u32[]{:S(2)}) copy-start(f32[256]{0:T(256)S(1)} %add_rsqrt_fusion.1) | copy-start | bytes 3076
  113.9 9.7 %slice-start.4 = ((s8[4718592]{0:T(1024)(128)(4,1)}), s8[524288]{0:T(1024)(128)(4,1)S(1)}, s32[]{:S(2)}) async-start(s8[4718592]{0:T(1024)(128)(4,1)} %bitcast.136), calls=%async_computation.5 | async-start | bytes 1048576
  125.2 5.9 copy-start.3
  125.2 5.9 copy-start.39
  125.5 5.6 copy-start.44
  125.5 5.7 slice-start.5
  127.3 3.9 slice-start.6
  156.3 2.4 collective-permute-start.8
  165.9 18.3 %copy-start.54 = (pred[200]{0:T(512)(128)(4,1)S(1)}, pred[200]{0:T(512)(128)(4,1)}, u32[]{:S(2)}) copy-start(pred[200]{0:T(512)(128)(4,1)} %copy-done.53) | copy-start | bytes 604
  165.9 18.3 %copy-start.56 = (pred[200]{0:T(512)(128)(4,1)S(1)}, pred[200]{0:T(512)(128)(4,1)}, u32[]{:S(2)}) copy-start(pred[200]{0:T(512)(128)(4,1)} %copy-done.55) | copy-start | bytes 604
  167.4 11.6 %collective-permute-start.9 = (f32[2,200,256]{2,1,0:T(8,128)S(1)}, f32[2,200,256]{2,1,0:T(8,128)S(1)}, u32[]{:S(2)}, u32[]{:S(2)}) collective-permute-start(f32[2,200,256]{2,1,0:T(8,128)S(1)} %constant_dynamic-slice_fusion), channel_id=1, source_target_pairs={{0,2},{1,3},{2,0},{3,1},{4,6},{5,7},{6,4},{7,5},{8,10},{9,11},{10,... | collective-permute-start | bytes 1228808 | tf_op jit(solution)/shard_map/ppermute | solution.py:256
  179.1 39.4 %copy-start.32 = (f32[768]{0:T(1024)S(1)}, f32[768]{0:T(1024)}, u32[]{:S(2)}) copy-start(f32[768]{0:T(1024)} %param.23) | copy-start | bytes 9220
  179.1 39.4 %copy-start.34 = (f32[768]{0:T(1024)S(1)}, f32[768]{0:T(1024)}, u32[]{:S(2)}) copy-start(f32[768]{0:T(1024)} %param.24) | copy-start | bytes 9220
  179.1 39.4 %copy-start.36 = (f32[256]{0:T(256)S(1)}, f32[256]{0:T(256)}, u32[]{:S(2)}) copy-start(f32[256]{0:T(256)} %copy-done.35) | copy-start | bytes 3076
  179.1 39.4 %copy-start.43 = (f32[256]{0:T(256)S(1)}, f32[256]{0:T(256)}, u32[]{:S(2)}) copy-start(f32[256]{0:T(256)} %copy-done.42) | copy-start | bytes 3076
  186.4 17.9 %collective-permute-start.13 = (f32[200,256]{1,0:T(8,128)}, f32[200,256]{1,0:T(8,128)}, u32[]{:S(2)}, u32[]{:S(2)}) collective-permute-start(f32[200,256]{1,0:T(8,128)} %get-tuple-element.127), channel_id=1, source_target_pairs={{8,0},{9,1},{10,2},{11,3},{12,4},{13,5},{14,6},{15,7},{24,16},{25,... | collective-permute-start | bytes 614408 | tf_op jit(solution)/shard_map/ppermute | solution.py:305
  187.7 19.0 %collective-permute-start.12 = (f32[200,256]{1,0:T(8,128)}, f32[200,256]{1,0:T(8,128)}, u32[]{:S(2)}, u32[]{:S(2)}) collective-permute-start(f32[200,256]{1,0:T(8,128)} %get-tuple-element.127), channel_id=1, source_target_pairs={{4,0},{5,1},{6,2},{7,3},{8,4},{9,5},{10,6},{11,7},{12,8},{13,9},{1... | collective-permute-start | bytes 614408 | tf_op jit(solution)/shard_map/ppermute | solution.py:305
  189.0 20.3 %collective-permute-start.11 = (f32[200,256]{1,0:T(8,128)S(1)}, f32[200,256]{1,0:T(8,128)}, u32[]{:S(2)}, u32[]{:S(2)}) collective-permute-start(f32[200,256]{1,0:T(8,128)S(1)} %get-tuple-element.126), channel_id=1, source_target_pairs={{0,8},{1,9},{2,10},{3,11},{4,12},{5,13},{6,14},{7,15},{16,24},{17,... | collective-permute-start | bytes 614408 | tf_op jit(solution)/shard_map/ppermute | solution.py:304
  196.4 15.4 %collective-permute-start.10 = (f32[200,256]{1,0:T(8,128)S(1)}, f32[200,256]{1,0:T(8,128)}, u32[]{:S(2)}, u32[]{:S(2)}) collective-permute-start(f32[200,256]{1,0:T(8,128)S(1)} %get-tuple-element.126), channel_id=1, source_target_pairs={{0,4},{1,5},{2,6},{3,7},{4,8},{5,9},{6,10},{7,11},{8,12},{9,13},{1... | collective-permute-start | bytes 614408 | tf_op jit(solution)/shard_map/ppermute | solution.py:304
  214.3 4.2 copy-start.30
  217.0 6.8 copy-start.25
  217.1 11.4 %collective-permute-start.14 = (f32[2,200,256]{2,1,0:T(8,128)}, f32[2,200,256]{2,1,0:T(8,128)}, u32[]{:S(2)}, u32[]{:S(2)}) collective-permute-start(f32[2,200,256]{2,1,0:T(8,128)} %fusion.29), channel_id=1, source_target_pairs={{0,2},{1,3},{2,0},{3,1},{4,6},{5,7},{6,4},{7,5},{8,10},{9,11},{10,... | collective-permute-start | bytes 1228808 | tf_op jit(solution)/shard_map/ppermute | solution.py:256
  223.9 4.5 copy-start.18
  223.9 5.8 copy-start.6
  230.1 8.1 %collective-permute-start.15 = (f32[2,400,256]{2,1,0:T(8,128)S(1)}, f32[2,400,256]{2,1,0:T(8,128)S(1)}, u32[]{:S(2)}, u32[]{:S(2)}) collective-permute-start(f32[2,400,256]{2,1,0:T(8,128)S(1)} %fusion.20), channel_id=1, source_target_pairs={{0,1},{1,0},{2,3},{3,2},{4,5},{5,4},{6,7},{7,6},{8,9},{9,8},{10,11... | collective-permute-start | bytes 2457608 | tf_op jit(solution)/shard_map/ppermute | solution.py:256
  261.7 41.6 %copy-start.7 = (bf16[768,768]{1,0:T(8,128)(2,1)S(1)}, bf16[768,768]{1,0:T(8,128)(2,1)}, u32[]{:S(2)}) copy-start(bf16[768,768]{1,0:T(8,128)(2,1)} %wq_ref.1) | copy-start | bytes 3538948
  261.7 43.3 %copy-start.8 = (bf16[768,768]{1,0:T(8,128)(2,1)S(1)}, bf16[768,768]{1,0:T(8,128)(2,1)}, u32[]{:S(2)}) copy-start(bf16[768,768]{1,0:T(8,128)(2,1)} %wk_ref.1) | copy-start | bytes 3538948
  261.8 43.2 %copy-start.26 = (bf16[256,768]{1,0:T(8,128)(2,1)S(1)}, bf16[256,768]{1,0:T(8,128)(2,1)}, u32[]{:S(2)}) copy-start(bf16[256,768]{1,0:T(8,128)(2,1)} %get-tuple-element.32) | copy-start | bytes 1179652
  699.7 10.7 %slice-start = ((s8[9437184]{0:T(1024)(128)(4,1)}), s8[4194304]{0:T(1024)(128)(4,1)S(1)}, s32[]{:S(2)}) async-start(s8[9437184]{0:T(1024)(128)(4,1)} %bitcast.134), calls=%async_computation.1 | async-start | bytes 8388608
  701.1 9.3 %slice-start.1 = ((s8[9437184]{0:T(1024)(128)(4,1)}), s8[4194304]{0:T(1024)(128)(4,1)S(1)}, s32[]{:S(2)}) async-start(s8[9437184]{0:T(1024)(128)(4,1)} %bitcast.134), calls=%async_computation.2 | async-start | bytes 8388608
  701.1 9.3 %slice-start.2 = ((s8[9437184]{0:T(1024)(128)(4,1)}), s8[1048576]{0:T(1024)(128)(4,1)S(1)}, s32[]{:S(2)}) async-start(s8[9437184]{0:T(1024)(128)(4,1)} %bitcast.134), calls=%async_computation.3 | async-start | bytes 2097152
  (33 other events, 67.1 us)
Sparse Core Ops, SparseCore 0:
  261.8 429.4 all-reduce.3
